TPU v7x, 32 devices: a whole 2x2x4 slice. The times are simulated.
32 devices in a mesh: dp: 8 (over y, x, core), mp: 4 (over z).
Axes of the slice: x: 2, y: 2, z: 4, core: 2. Of those that a mesh axis runs over, the one named last changes fastest.
Arguments:
- tokens: bfloat16 [8, 2048, 512], P('dp', 'mp'), may hold values from -6 to 6
- cotangent: bfloat16 [8, 2048, 512], P('dp', 'mp'), may hold values from -6 to 6
- lengths: int32 [8], P('dp'), may hold values from 512 to 2048, as said below
- owners: int32 [96], replicated, may hold values from 0 to 7, as said below
- w_qkv: bfloat16 [512, 1536], P(None, 'mp'), may hold values from -0.25 to 0.25
- w_out: bfloat16 [512, 512], P('mp'), may hold values from -0.75 to 0.75
- w_in: bfloat16 [512, 2048], P(None, 'mp'), may hold values from -0.25 to 0.25
- w_down: bfloat16 [2048, 512], P('mp'), may hold values from -0.125 to 0.125
- master: float32 [192, 256, 128], P('dp', 'mp'), may hold values from -0.75 to 0.75
- first_moment: float32 [192, 256, 128], P('dp', 'mp'), may hold values from -28 to 28
- second_moment: float32 [192, 256, 128], P('dp', 'mp'), may hold values from 49.152 to 409.6
- norm_gains: float32 [2, 512], replicated, may hold values from 0.25 to 1.75
- norm_biases: float32 [2, 512], replicated, may hold values from -1.5 to 1.5
- norm_first: float32 [4, 512], replicated, may hold values from -64 to 64
- norm_second: float32 [4, 512], replicated, may hold values from 262.144 to 2064.384
Outputs:
- outputs: bfloat16 [8, 2048, 512], P('dp', 'mp')
- tokens_grad: float32 [8, 2048, 512], P('dp', 'mp')
- first_new: float32 [192, 256, 128], P('dp', 'mp')
- second_new: float32 [192, 256, 128], P('dp', 'mp')
- master_new: float32 [192, 256, 128], P('dp', 'mp')
- new_qkv: bfloat16 [512, 1536], P(None, 'mp')
- new_out: bfloat16 [512, 512], P('mp')
- new_in: bfloat16 [512, 2048], P(None, 'mp')
- new_down: bfloat16 [2048, 512], P('mp')
- norm_first_new: float32 [4, 512], replicated
- norm_second_new: float32 [4, 512], replicated
- norm_new: float32 [4, 512], replicated
Inputs may be any that keep to these rules, and one draw needn't show every extreme that they name: `lengths`: one sequence in every draw has all 2048 positions valid. `owners`: no owner holds more than 24 blocks and one owner holds exactly 24.
All inputs are finite; a program needn't handle non-finite values.
Results may differ from a plain program's by a relative error of at most 0.0097.
Values may be sent and summed in bfloat16 or wider, within the bound.
No kernel may reach another device: no remote copies, remote signals or barrier semaphores. Data moves between devices by JAX's collectives and lax.ppermute only.
A program may use at most 128 MiB of HBM per device.

v0:
```python
import jax
import jax.numpy as jnp
from jax import lax
from jax.sharding import PartitionSpec as P

HEAD = 64
BAND = 30
MARGIN = 32
QBLOCK = 512
STEP = 10
highest = lax.Precision.HIGHEST
learn_rate = 0.1
norm_rate = 0.3
decay_rate = 0.1
beta_one = 0.9
beta_two = 0.95
adam_epsilon = 1e-08
norm_epsilon = 1e-05


def layer_norm(values, scale_gain, shift_bias):
    row_mean = jnp.mean(values, axis=-1, keepdims=True)
    centered = values - row_mean
    variance = jnp.mean(centered * centered, axis=-1, keepdims=True)
    return centered * lax.rsqrt(variance + norm_epsilon) * scale_gain + shift_bias


def far_field(query, keys, values, key_mask, valid_count):
    masked = key_mask[:, None, None]
    feat_keys = (jax.nn.elu(keys) + 1.0) * masked
    tanh_keys = jnp.tanh(keys) * masked
    feat_query = jax.nn.elu(query) + 1.0
    tanh_query = jnp.tanh(query)
    state_one = jnp.einsum("lhe,lhf->hef", feat_keys, values, precision=highest)
    normaliser = jnp.sum(feat_keys, axis=0)
    denominator = jnp.einsum("lhe,he->lh", feat_query, normaliser, precision=highest)
    first_part = (
        jnp.einsum("lhe,hef->lhf", feat_query, state_one, precision=highest)
        / denominator[:, :, None]
    )
    state_two = jnp.einsum("lhe,lhf->hef", tanh_keys, values, precision=highest) / valid_count
    return first_part + jnp.einsum("lhe,hef->lhf", tanh_query, state_two, precision=highest)


def band_mask(anchor, length, seq_len, block):
    query_pos = anchor + jnp.arange(block, dtype=jnp.int32)
    key_pos = anchor - MARGIN + jnp.arange(block + 2 * MARGIN, dtype=jnp.int32)
    offsets = query_pos[:, None] - key_pos[None, :]
    inside = (key_pos >= 0) & (key_pos < seq_len)
    return (
        (jnp.abs(offsets) <= BAND)
        & inside[None, :]
        & ((key_pos < length)[None, :] | (offsets == 0))
    )


def cross(left, right):
    return lax.dot_general(
        left, right, (((0,), (0,)), ((), ())), preferred_element_type=jnp.float32
    )


def against(left, right):
    return lax.dot_general(
        left, right, (((1,), (1,)), ((), ())), preferred_element_type=jnp.float32
    )


def block_scores(query_blk, key_blk, anchor, length, seq_len, block):
    scores = (
        jnp.einsum("qhe,khe->hqk", query_blk, key_blk, preferred_element_type=jnp.float32) * 0.125
    )
    return jnp.where(band_mask(anchor, length, seq_len, block)[None], scores, -1e30)


def near_forward(query, key_pad, value_pad, length, seq_len, base, block):
    rows = query.shape[0]
    span = block + 2 * MARGIN

    def window(anchor):
        query_blk = lax.dynamic_slice_in_dim(query, anchor, block, 0)
        key_blk = lax.dynamic_slice_in_dim(key_pad, anchor, span, 0)
        value_blk = lax.dynamic_slice_in_dim(value_pad, anchor, span, 0)
        scores = block_scores(query_blk, key_blk, base + anchor, length, seq_len, block)
        row_max = jnp.max(scores, axis=-1, keepdims=True)
        exponent = jnp.exp(scores - row_max)
        summed = jnp.sum(exponent, axis=-1, keepdims=True)
        attn_probs = (exponent / summed).astype(jnp.bfloat16)
        result = jnp.einsum(
            "hqk,khe->qhe", attn_probs, value_blk, preferred_element_type=jnp.float32
        )
        return (result, (row_max + jnp.log(summed))[:, :, 0])

    anchors = jnp.arange(rows // block, dtype=jnp.int32) * block
    results, log_sums = lax.map(window, anchors)
    return (results.reshape(query.shape), log_sums)


def near_backward(query, key_pad, value_pad, grad_ctx, log_sums, length, seq_len, base, block):
    rows = query.shape[0]
    span = block + 2 * MARGIN
    padded_shape = key_pad.shape

    def visit(block_index, running):
        grad_query, grad_keys, grad_values = running
        anchor = block_index * block
        query_blk = lax.dynamic_slice_in_dim(query, anchor, block, 0)
        key_blk = lax.dynamic_slice_in_dim(key_pad, anchor, span, 0)
        value_blk = lax.dynamic_slice_in_dim(value_pad, anchor, span, 0)
        grad_blk = lax.dynamic_slice_in_dim(grad_ctx, anchor, block, 0)
        scores = block_scores(query_blk, key_blk, base + anchor, length, seq_len, block)
        attn_probs = jnp.exp(scores - log_sums[block_index][:, :, None])
        probs_low = attn_probs.astype(jnp.bfloat16)
        grad_probs = jnp.einsum(
            "qhe,khe->hqk", grad_blk, value_blk, preferred_element_type=jnp.float32
        )
        row_dot = jnp.sum(attn_probs * grad_probs, axis=-1, keepdims=True)
        grad_scores = (attn_probs * (grad_probs - row_dot)).astype(jnp.bfloat16)
        query_part = (
            jnp.einsum("hqk,khe->qhe", grad_scores, key_blk, preferred_element_type=jnp.float32)
            * 0.125
        )
        key_part = (
            jnp.einsum("hqk,qhe->khe", grad_scores, query_blk, preferred_element_type=jnp.float32)
            * 0.125
        )
        value_part = jnp.einsum(
            "hqk,qhe->khe", probs_low, grad_blk, preferred_element_type=jnp.float32
        )
        grad_query = lax.dynamic_update_slice_in_dim(grad_query, query_part, anchor, 0)
        grad_keys = lax.dynamic_update_slice_in_dim(
            grad_keys, lax.dynamic_slice_in_dim(grad_keys, anchor, span, 0) + key_part, anchor, 0
        )
        grad_values = lax.dynamic_update_slice_in_dim(
            grad_values,
            lax.dynamic_slice_in_dim(grad_values, anchor, span, 0) + value_part,
            anchor,
            0,
        )
        return (grad_query, grad_keys, grad_values)

    initial = (
        jnp.zeros(query.shape, jnp.float32),
        jnp.zeros(padded_shape, jnp.float32),
        jnp.zeros(padded_shape, jnp.float32),
    )
    return lax.fori_loop(0, rows // block, visit, initial)


def per_device(
    tokens,
    cotangent,
    lengths,
    owners,
    w_qkv,
    w_out,
    w_in,
    w_down,
    master,
    first_moment,
    second_moment,
    norm_gains,
    norm_biases,
    norm_first,
    norm_second,
):
    inputs = tokens[0].astype(jnp.float32)
    local_rows = inputs.shape[0]
    groups = lax.axis_size("mp")
    seq_len = local_rows * groups
    length = lengths[0]
    base = lax.axis_index("mp") * local_rows
    row_pos = base + jnp.arange(local_rows, dtype=jnp.int32)
    grad_output = cotangent[0].astype(jnp.float32) * (row_pos < length).astype(jnp.float32)[:, None]
    head_cols = w_out.shape[0]
    heads_dev = head_cols // HEAD
    valid_count = length.astype(jnp.float32)
    grad_mix = grad_output.astype(jnp.bfloat16)
    norm_one, norm_one_back = jax.vjp(layer_norm, inputs, norm_gains[0], norm_biases[0])
    first_local = norm_one.astype(jnp.bfloat16)
    first_all = lax.all_gather(first_local, "mp", axis=0, tiled=True)
    projected = jnp.dot(first_all, w_qkv, preferred_element_type=jnp.float32).astype(jnp.bfloat16)
    query = projected[:, :head_cols].reshape(seq_len, heads_dev, HEAD)
    keys = projected[:, head_cols : 2 * head_cols].reshape(seq_len, heads_dev, HEAD)
    values = projected[:, 2 * head_cols :].reshape(seq_len, heads_dev, HEAD)
    key_mask = (jnp.arange(seq_len, dtype=jnp.int32) < length).astype(jnp.float32)
    key_pad = jnp.pad(keys, ((MARGIN, MARGIN), (0, 0), (0, 0)))
    value_pad = jnp.pad(values, ((MARGIN, MARGIN), (0, 0), (0, 0)))
    near_part, log_sums = near_forward(query, key_pad, value_pad, length, seq_len, 0, QBLOCK)

    def far_local(query_f, keys_f, values_f):
        return far_field(query_f, keys_f, values_f, key_mask, valid_count)

    far_part, far_back = jax.vjp(
        far_local, query.astype(jnp.float32), keys.astype(jnp.float32), values.astype(jnp.float32)
    )
    context = (near_part + far_part).reshape(seq_len, head_cols).astype(jnp.bfloat16)
    second_in = inputs + lax.psum_scatter(
        jnp.dot(context, w_out, preferred_element_type=jnp.float32),
        "mp",
        scatter_dimension=0,
        tiled=True,
    )
    norm_two, norm_two_back = jax.vjp(layer_norm, second_in, norm_gains[1], norm_biases[1])
    second_local = norm_two.astype(jnp.bfloat16)
    second_all = lax.all_gather(second_local, "mp", axis=0, tiled=True)
    pre_act = jnp.dot(second_all, w_in, preferred_element_type=jnp.float32)
    activated, gelu_back = jax.vjp(jax.nn.gelu, pre_act)
    hidden = activated.astype(jnp.bfloat16)
    result = second_in + lax.psum_scatter(
        jnp.dot(hidden, w_down, preferred_element_type=jnp.float32),
        "mp",
        scatter_dimension=0,
        tiled=True,
    )
    portion = lax.all_gather(grad_mix, "mp", axis=0, tiled=True)
    grad_hidden = against(portion, w_down)
    grad_hidden, grad_down = (grad_hidden, cross(hidden, portion))
    grad_up = gelu_back(grad_hidden)[0].astype(jnp.bfloat16)
    grad_norm_two = lax.psum_scatter(against(grad_up, w_in), "mp", scatter_dimension=0, tiled=True)
    grad_inw = cross(second_all, grad_up)
    grad_second, grad_gain_two, grad_bias_two = norm_two_back(grad_norm_two)
    grad_second = grad_output + grad_second
    grad_attn = grad_second.astype(jnp.bfloat16)
    portion = lax.all_gather(grad_attn, "mp", axis=0, tiled=True)
    grad_context = against(portion, w_out)
    grad_context, grad_outw = (grad_context, cross(context, portion))
    grad_context = grad_context.astype(jnp.bfloat16).reshape(seq_len, heads_dev, HEAD)
    near_query, near_keys_pad, near_values_pad = near_backward(
        query, key_pad, value_pad, grad_context, log_sums, length, seq_len, 0, QBLOCK
    )
    near_keys = near_keys_pad[MARGIN : MARGIN + seq_len]
    near_values = near_values_pad[MARGIN : MARGIN + seq_len]
    far_query, far_keys, far_values = far_back(grad_context.astype(jnp.float32))
    grad_proj = jnp.concatenate(
        [
            (near_query + far_query).reshape(seq_len, head_cols),
            (near_keys + far_keys).reshape(seq_len, head_cols),
            (near_values + far_values).reshape(seq_len, head_cols),
        ],
        axis=1,
    ).astype(jnp.bfloat16)
    grad_norm_one = lax.psum_scatter(
        against(grad_proj, w_qkv), "mp", scatter_dimension=0, tiled=True
    )
    grad_qkvw = cross(first_all, grad_proj)
    block_rows = master.shape[1]
    grad_blocks = jnp.concatenate(
        [
            grad_qkvw.reshape(-1, 128),
            grad_outw.reshape(-1, 128),
            grad_inw.reshape(-1, 128),
            grad_down.reshape(-1, 128),
        ],
        axis=0,
    ).reshape(owners.shape[0], block_rows, 128)
    grad_first, grad_gain_one, grad_bias_one = norm_one_back(grad_norm_one)
    tokens_grad = grad_second + grad_first
    corr_one = 1.0 - beta_one**STEP
    corr_two = 1.0 - beta_two**STEP
    norm_grad = lax.psum(
        jnp.stack([grad_gain_one, grad_bias_one, grad_gain_two, grad_bias_two]), ("dp", "mp")
    )
    norm_params = jnp.stack([norm_gains[0], norm_biases[0], norm_gains[1], norm_biases[1]])
    norm_first_new = beta_one * norm_first + (1.0 - beta_one) * norm_grad
    norm_second_new = beta_two * norm_second + (1.0 - beta_two) * norm_grad * norm_grad
    norm_new = norm_params - norm_rate * (
        norm_first_new / corr_one / (jnp.sqrt(norm_second_new / corr_two) + adam_epsilon)
    )
    block_rows = master.shape[1]
    capacity = master.shape[0]
    blocks_all = owners.shape[0]
    dp_count = lax.axis_size("dp")
    onehot = (owners[:, None] == jnp.arange(dp_count, dtype=jnp.int32)[None, :]).astype(jnp.int32)
    slot_index = jnp.sum(jnp.cumsum(onehot, axis=0) * onehot, axis=1) - 1
    slot_rows = owners * capacity + slot_index
    my_rows = lax.axis_index("dp") * capacity + jnp.arange(capacity, dtype=jnp.int32)
    matches = slot_rows[None, :] == my_rows[:, None]
    filled = jnp.any(matches, axis=1)
    picked = jnp.sum(
        jnp.where(matches, jnp.arange(blocks_all, dtype=jnp.int32)[None, :], 0), axis=1
    )
    summed = lax.psum(grad_blocks, "dp")
    owned = summed[picked]
    first_upd = beta_one * first_moment + (1.0 - beta_one) * owned
    second_upd = beta_two * second_moment + (1.0 - beta_two) * owned * owned
    master_upd = master - learn_rate * (
        first_upd / corr_one / (jnp.sqrt(second_upd / corr_two) + adam_epsilon)
        + decay_rate * master
    )
    keep_mask = filled[:, None, None]
    first_new = jnp.where(keep_mask, first_upd, first_moment)
    second_new = jnp.where(keep_mask, second_upd, second_moment)
    master_new = jnp.where(keep_mask, master_upd, master)
    gathered = lax.all_gather(master_new.astype(jnp.bfloat16), "dp", axis=0, tiled=True)
    fresh = gathered[slot_rows].reshape(blocks_all * block_rows, 128)
    rows_q = w_qkv.size // 128
    rows_o = w_out.size // 128
    rows_i = w_in.size // 128
    new_qkv = fresh[:rows_q].reshape(w_qkv.shape)
    new_out = fresh[rows_q : rows_q + rows_o].reshape(w_out.shape)
    new_in = fresh[rows_q + rows_o : rows_q + rows_o + rows_i].reshape(w_in.shape)
    new_down = fresh[rows_q + rows_o + rows_i :].reshape(w_down.shape)
    return (
        result.astype(jnp.bfloat16)[None],
        tokens_grad[None],
        first_new,
        second_new,
        master_new,
        new_qkv,
        new_out,
        new_in,
        new_down,
        norm_first_new,
        norm_second_new,
        norm_new,
    )


def solution(mesh):
    return jax.shard_map(
        per_device,
        mesh=mesh,
        in_specs=(
            P("dp", "mp", None),
            P("dp", "mp", None),
            P("dp"),
            P(),
            P(None, "mp"),
            P("mp", None),
            P(None, "mp"),
            P("mp", None),
            P("dp", "mp", None),
            P("dp", "mp", None),
            P("dp", "mp", None),
            P(),
            P(),
            P(),
            P(),
        ),
        out_specs=(
            P("dp", "mp", None),
            P("dp", "mp", None),
            P("dp", "mp", None),
            P("dp", "mp", None),
            P("dp", "mp", None),
            P(None, "mp"),
            P("mp", None),
            P(None, "mp"),
            P("mp", None),
            P(),
            P(),
            P(),
        ),
        check_vma=False,
    )
```

profile of v0, /device:TPU:0, one launch (start us, length us, event | category | flops | bytes accessed | tf_op | source)
XLA Modules:
  0.0 864.3 jit_solution(8731403079336793505)
XLA Ops:
  13.6 48.1 %all-gather.6.cloned.1.call-done = bf16[2048,512]{1,0:T(8,128)(2,1)} async-done(((bf16[512,512]{1,0:T(8,128)(2,1)}), bf16[2048,512]{1,0:T(8,128)(2,1)}) %all-gather.6.cloned.1.call-update) | async-done | bytes 2097168 | tf_op jit(solution)/shard_map/all_gather | solution.py:181
  70.3 66.4 %while.33 = (s32[]{:T(128)}, f32[4,512,2,64]{1,0,3,2:T(4,128)}, f32[4,2,512]{2,1,0:T(2,128)}, s32[4]{0:T(128)S(1)}, bf16[2112,2,64]{0,2,1:T(8,128)(2,1)S(1)}, /*...) while((s32[]{:T(128)}, f32[4,512,2,64]{1,0,3,2:T(4,128)}, ...), condition=%wide.region_5.6_spmd, body=%wide.region_2.5_spmd.sunk | while | flops 160140160 | bytes 10071036 | solution.py:95
  80.7 6.1 dynamic_update_slice.52
  97.3 6.1 dynamic_update_slice.52
  113.9 6.1 dynamic_update_slice.52
  130.5 6.1 dynamic_update_slice.52
  151.2 73.6 %reduce-scatter.5.cloned.1.call-done = f32[512,512]{1,0:T(8,128)} async-done(((f32[2048,512]{1,0:T(8,128)}), f32[512,512]{1,0:T(8,128)}) %reduce-scatter.5.cloned.1.call-update) | async-done | bytes 1048592 | tf_op jit(solution)/shard_map/reduce_scatter | solution.py:198
  227.5 45.9 %all-gather.10.cloned.1.call-done = bf16[2048,512]{1,0:T(8,128)(2,1)} async-done(((bf16[512,512]{1,0:T(8,128)(2,1)}), bf16[2048,512]{1,0:T(8,128)(2,1)}) %all-gather.10.cloned.1.call-update) | async-done | bytes 2097168 | tf_op jit(solution)/shard_map/all_gather | solution.py:216
  273.4 4.8 fusion.198
  278.3 41.9 %all-gather.8.cloned.1.call-done = bf16[2048,512]{1,0:T(8,128)(2,1)} async-done(((bf16[512,512]{1,0:T(8,128)(2,1)}), bf16[2048,512]{1,0:T(8,128)(2,1)}) %all-gather.8.cloned.1.call-update) | async-done | bytes 2097168 | tf_op jit(solution)/shard_map/all_gather | solution.py:206
  320.2 6.9 fusion.53
  331.8 5.9 fusion.187
  337.8 69.6 %reduce-scatter.9.cloned.1.call-done = f32[512,512]{1,0:T(8,128)} async-done(((f32[2048,512]{1,0:T(8,128)}), f32[512,512]{1,0:T(8,128)}) %reduce-scatter.9.cloned.1.call-update) | async-done | bytes 1048592 | tf_op jit(solution)/shard_map/reduce_scatter | solution.py:220
  409.6 77.2 %reduce-scatter.7.cloned.1.call-done = f32[512,512]{1,0:T(8,128)} async-done(((f32[2048,512]{1,0:T(8,128)}), f32[512,512]{1,0:T(8,128)}) %reduce-scatter.7.cloned.1.call-update) | async-done | bytes 1048592 | tf_op jit(solution)/shard_map/reduce_scatter | solution.py:210
  496.8 4.9 fusion.186
  502.7 34.5 %all-gather.12.cloned.1.call-done = bf16[2048,512]{1,0:T(8,128)(2,1)} async-done(((bf16[512,512]{1,0:T(8,128)(2,1)}), bf16[2048,512]{1,0:T(8,128)(2,1)}) %all-gather.12.cloned.1.call-update) | async-done | bytes 2097168 | tf_op jit(solution)/shard_map/all_gather | solution.py:225
  549.5 50.3 %while.34 = (s32[]{:T(128)}, f32[2048,2,64]{0,2,1:T(8,128)}, f32[2112,2,64]{0,2,1:T(8,128)}, f32[2112,2,64]{0,2,1:T(8,128)S(1)}, bf16[2112,2,64]{0,2,1:T(8,128)(...) while((s32[]{:T(128)}, f32[2048,2,64]{0,2,1:T(8,128)}, ...), condition=%wide.region_16.17_spmd, body=%wide.region_14.16_spmd.sunk | while | flops 385149824 | bytes 24149072 | solution.py:147
  624.2 66.9 %all-reduce.4.cloned.1.call-done = f32[96,64,128]{2,1,0:T(8,128)} async-done(((f32[96,64,128]{2,1,0:T(8,128)}), f32[96,64,128]{2,1,0:T(8,128)}) %all-reduce.4.cloned.1.call-update) | async-done | bytes 3145744 | tf_op jit(solution)/shard_map/psum | solution.py:283
  693.6 4.2 fusion.189
  698.2 4.5 fusion.140
  702.7 27.7 %all-gather.14.cloned.1.call-done = bf16[192,64,128]{2,1,0:T(8,128)(2,1)} async-done(((bf16[24,64,128]{2,1,0:T(8,128)(2,1)}), bf16[192,64,128]{2,1,0:T(8,128)(2,1)}) %all-gather.14.cloned.1.call-update) | async-done | bytes 3145744 | tf_op jit(solution)/shard_map/all_gather | solution.py:295
  730.3 3.9 gather_fusion.1
  740.5 68.8 %reduce-scatter.11.cloned.1.call-done = f32[512,512]{1,0:T(8,128)} async-done(((f32[2048,512]{1,0:T(8,128)}), f32[512,512]{1,0:T(8,128)}) %reduce-scatter.11.cloned.1.call-update) | async-done | bytes 1048592 | tf_op jit(solution)/shard_map/reduce_scatter | solution.py:243
  812.9 40.8 %psum.15 = f32[4,512]{1,0:T(4,128)S(1)} all-reduce(f32[4,512]{1,0:T(4,128)S(1)} %pad_maximum_fusion.4), channel_id=1, replica_groups=mesh['dp'=8,'mp'=4] {'dp','mp'}, use_global_device_ids=true, to_apply=%region_30.31 | all-reduce | flops 2048 | bytes 16384 | tf_op jit(solution)/shard_map/psum | solution.py:261
  (319 shorter events, 177.2 us)
Async XLA Ops:
  7.2 313.0 %copy-start = (bf16[512,512]{1,0:T(8,128)(2,1)S(1)}, bf16[512,512]{1,0:T(8,128)(2,1)}, u32[]{:S(2)}) copy-start(bf16[512,512]{1,0:T(8,128)(2,1)} %param.25) | copy-start | bytes 1572868
  7.2 54.4 %all-gather.6.cloned.1.call-start = ((), (), s32[]{:S(2)}) async-start(), calls=%async_computation.4 | async-start | bytes 2621440 | tf_op jit(solution)/shard_map/all_gather | solution.py:181
  10.7 215.7 %copy-start.35 = (f32[1,512]{1,0:T(1,128)}, f32[1,512]{1,0:T(1,128)S(1)}, u32[]{:S(2)}) copy-start(f32[1,512]{1,0:T(1,128)S(1)} %get-tuple-element.443) | copy-start | bytes 6148
  10.7 476.1 %copy-start.25 = (f32[1,512]{1,0:T(1,128)}, f32[1,512]{1,0:T(1,128)S(1)}, u32[]{:S(2)}) copy-start(f32[1,512]{1,0:T(1,128)S(1)} %get-tuple-element.434) | copy-start | bytes 6148
  12.8 211.9 %reduce-scatter.5.cloned.1.call-start = ((), (), s32[]{:S(2)}) async-start(), calls=%async_computation.5 | async-start | bytes 5242880 | tf_op jit(solution)/shard_map/reduce_scatter | solution.py:198
  149.1 75.7 %copy-start.2 = (bf16[1,512,512]{2,1,0:T(8,128)(2,1)S(1)}, bf16[1,512,512]{2,1,0:T(8,128)(2,1)}, u32[]{:S(2)}) copy-start(bf16[1,512,512]{2,1,0:T(8,128)(2,1)} %param.19) | copy-start | bytes 1572868
  149.1 124.3 %all-gather.10.cloned.1.call-start = ((), (), s32[]{:S(2)}) async-start(), calls=%async_computation.8 | async-start | bytes 2621440 | tf_op jit(solution)/shard_map/all_gather | solution.py:216
  150.1 339.5 %copy-start.29 = (f32[512]{0:T(512)}, f32[512]{0:T(512)S(1)}, u32[]{:S(2)}) copy-start(f32[512]{0:T(512)S(1)} %fusion.167) | copy-start | bytes 6148
  151.1 122.3 %copy-start.20 = (bf16[512,512]{1,0:T(8,128)(2,1)S(1)}, bf16[512,512]{1,0:T(8,128)(2,1)}, u32[]{:S(2)}) copy-start(bf16[512,512]{1,0:T(8,128)(2,1)} %param.26) | copy-start | bytes 1572868
  151.1 169.1 %all-gather.8.cloned.1.call-start = ((), (), s32[]{:S(2)}) async-start(), calls=%async_computation.6 | async-start | bytes 2621440 | tf_op jit(solution)/shard_map/all_gather | solution.py:206
  227.5 179.9 %reduce-scatter.9.cloned.1.call-start = ((), (), s32[]{:S(2)}) async-start(), calls=%async_computation.9 | async-start | bytes 5242880 | tf_op jit(solution)/shard_map/reduce_scatter | solution.py:220
  331.7 155.1 %reduce-scatter.7.cloned.1.call-start = ((), (), s32[]{:S(2)}) async-start(), calls=%async_computation.7 | async-start | bytes 5242880 | tf_op jit(solution)/shard_map/reduce_scatter | solution.py:210
  337.7 199.5 %all-gather.12.cloned.1.call-start = ((), (), s32[]{:S(2)}) async-start(), calls=%async_computation.10 | async-start | bytes 2621440 | tf_op jit(solution)/shard_map/all_gather | solution.py:225
  409.6 80.0 %copy-start.11 = (bf16[1,512,512]{2,1,0:T(8,128)(2,1)S(1)}, bf16[1,512,512]{2,1,0:T(8,128)(2,1)}, u32[]{:S(2)}) copy-start(bf16[1,512,512]{2,1,0:T(8,128)(2,1)} %param.20) | copy-start | bytes 1572868
  490.7 200.4 %all-reduce.4.cloned.1.call-start = ((), (), s32[]{:S(2)}) async-start(), calls=%async_computation.12 | async-start | bytes 6291456 | tf_op jit(solution)/shard_map/psum | solution.py:283
  622.7 107.6 %all-gather.14.cloned.1.call-start = ((), (), s32[]{:S(2)}) async-start(), calls=%async_computation.13 | async-start | bytes 3538944 | tf_op jit(solution)/shard_map/all_gather | solution.py:295
  697.8 111.5 %reduce-scatter.11.cloned.1.call-start = ((), (), s32[]{:S(2)}) async-start(), calls=%async_computation.11 | async-start | bytes 5242880 | tf_op jit(solution)/shard_map/reduce_scatter | solution.py:243
  738.4 115.3 %copy-start.26 = (f32[1,512]{1,0:T(1,128)S(1)}, f32[1,512]{1,0:T(1,128)}, u32[]{:S(2)}) copy-start(f32[1,512]{1,0:T(1,128)} %copy-done.25) | copy-start | bytes 6148
  738.4 115.3 %copy-start.34 = (f32[1,512]{1,0:T(1,128)S(1)}, f32[1,512]{1,0:T(1,128)}, u32[]{:S(2)}) copy-start(f32[1,512]{1,0:T(1,128)} %copy-done.33) | copy-start | bytes 6148
  738.4 115.3 %copy-start.36 = (f32[1,512]{1,0:T(1,128)S(1)}, f32[1,512]{1,0:T(1,128)}, u32[]{:S(2)}) copy-start(f32[1,512]{1,0:T(1,128)} %copy-done.35) | copy-start | bytes 6148
  738.4 115.3 %copy-start.42 = (f32[4,512]{1,0:T(4,128)S(1)}, f32[4,512]{1,0:T(4,128)}, u32[]{:S(2)}) copy-start(f32[4,512]{1,0:T(4,128)} %param.33) | copy-start | bytes 24580
  738.4 115.3 %copy-start.43 = (f32[4,512]{1,0:T(4,128)S(1)}, f32[4,512]{1,0:T(4,128)}, u32[]{:S(2)}) copy-start(f32[4,512]{1,0:T(4,128)} %param.32) | copy-start | bytes 24580
  739.3 115.0 %copy-start.30 = (f32[512]{0:T(512)S(1)}, f32[512]{0:T(512)}, u32[]{:S(2)}) copy-start(f32[512]{0:T(512)} %copy-done.29) | copy-start | bytes 6148
  739.3 115.0 %copy-start.38 = (f32[512]{0:T(512)S(1)}, f32[512]{0:T(512)}, u32[]{:S(2)}) copy-start(f32[512]{0:T(512)} %copy-done.37) | copy-start | bytes 6148
  (47 other events, 1018.0 us)
Sparse Core Ops, SparseCore 0:
  13.0 48.6 all-gather.5
  149.2 75.4 reduce-scatter.4
  227.0 46.4 all-gather.9
  275.5 44.6 all-gather.7
  331.9 75.4 reduce-scatter.8
  409.5 77.2 reduce-scatter.6
  490.8 46.3 all-gather.11
  622.9 68.1 all-reduce.3
  697.9 32.3 all-gather.13
  732.5 76.7 reduce-scatter.10
where the time goes:
time: 876 us; the launch traced here: 864 us
  waiting for transfers between devices  554 us (63%)
  matrix products  115 us (13%)
  local copies, waits for them, and re-layouts  69.2 us (8%)
  other arithmetic  51.3 us (6%)
  blocking collectives  40.8 us (5%)
  loops' own time  16.4 us (2%)
  between operations  16.1 us (2%)
    reduce_scatter x1, waiting for transfers between devices, per_device(): lax.psum_scatter(jnp.dot(hidden, w_down, preferred_element_type=jnp.float...  77.2 us
    reduce_scatter x1, waiting for transfers between devices, per_device(): lax.psum_scatter(jnp.dot(context, w_out, preferred_element_type=jnp.float...  73.6 us
    reduce_scatter x1, waiting for transfers between devices, per_device(): lax.psum_scatter(against(grad_up, w_in), 'mp', scatter_dimension=0, tiled...  69.6 us
    reduce_scatter x1, waiting for transfers between devices, per_device(): lax.psum_scatter(against(grad_proj, w_qkv), 'mp', scatter_dimension=0, ti...  68.8 us
    psum x1, waiting for transfers between devices, per_device(): summed = lax.psum(grad_blocks, 'dp')  66.9 us
    all_gather x1, waiting for transfers between devices, per_device(): first_all = lax.all_gather(first_local, 'mp', axis=0, tiled=True)  48.1 us
    all_gather x1, waiting for transfers between devices, per_device(): portion = lax.all_gather(grad_mix, 'mp', axis=0, tiled=True)  45.9 us
    all_gather x1, waiting for transfers between devices, per_device(): second_all = lax.all_gather(second_local, 'mp', axis=0, tiled=True)  41.9 us
  transfers between devices with their start and end apart: 10, of which 10 were waited for; matrix products, arithmetic and copies ran while one was open for 5% of the time, Pallas kernels for 0%

commit v1 on v0

--- a/solution.py
+++ b/solution.py
@@ -258,9 +258,9 @@
     tokens_grad = grad_second + grad_first
     corr_one = 1.0 - beta_one**STEP
     corr_two = 1.0 - beta_two**STEP
-    norm_grad = lax.psum(
-        jnp.stack([grad_gain_one, grad_bias_one, grad_gain_two, grad_bias_two]), ("dp", "mp")
-    )
+    block_2 = jnp.stack([grad_gain_one, grad_bias_one, grad_gain_two, grad_bias_two])
+    pieces = lax.all_gather(block_2, ("dp", "mp"))
+    norm_grad = jnp.sum(pieces, axis=0)
     norm_params = jnp.stack([norm_gains[0], norm_biases[0], norm_gains[1], norm_biases[1]])
     norm_first_new = beta_one * norm_first + (1.0 - beta_one) * norm_grad
     norm_second_new = beta_two * norm_second + (1.0 - beta_two) * norm_grad * norm_grad

time: 876 us -> 905 us (1.033)
  blocking collectives: 40.8 us -> 69.6 us
    all_gather x0 -> x1, blocking collectives: none -> 69.6 us  [per_device(): pieces = lax.all_gather(block_2, ('dp', 'mp'))]
    psum x1 -> x0, blocking collectives: 40.8 us -> none  [per_device(): lax.psum(jnp.stack([grad_gain_one, grad_bias_one, grad_gain_two, grad_bia...]
where the time goes in v1:
time: 905 us; the launch traced here: 893 us
  waiting for transfers between devices  554 us (61%)
  matrix products  115 us (13%)
  blocking collectives  69.6 us (8%)
  local copies, waits for them, and re-layouts  69.2 us (8%)
  other arithmetic  51.3 us (6%)
  loops' own time  16.4 us (2%)
  between operations  16.1 us (2%)
    reduce_scatter x1, waiting for transfers between devices, per_device(): lax.psum_scatter(jnp.dot(hidden, w_down, preferred_element_type=jnp.float...  77.2 us
    reduce_scatter x1, waiting for transfers between devices, per_device(): lax.psum_scatter(jnp.dot(context, w_out, preferred_element_type=jnp.float...  73.6 us
    all_gather x1, blocking collectives, per_device(): pieces = lax.all_gather(block_2, ('dp', 'mp'))  69.6 us
    reduce_scatter x1, waiting for transfers between devices, per_device(): lax.psum_scatter(against(grad_up, w_in), 'mp', scatter_dimension=0, tiled...  69.6 us
    reduce_scatter x1, waiting for transfers between devices, per_device(): lax.psum_scatter(against(grad_proj, w_qkv), 'mp', scatter_dimension=0, ti...  68.8 us
    psum x1, waiting for transfers between devices, per_device(): summed = lax.psum(grad_blocks, 'dp')  66.9 us
    all_gather x1, waiting for transfers between devices, per_device(): first_all = lax.all_gather(first_local, 'mp', axis=0, tiled=True)  48.1 us
    all_gather x1, waiting for transfers between devices, per_device(): portion = lax.all_gather(grad_mix, 'mp', axis=0, tiled=True)  45.9 us
  transfers between devices with their start and end apart: 10, of which 10 were waited for; matrix products, arithmetic and copies ran while one was open for 5% of the time, Pallas kernels for 0%

profile of v1, /device:TPU:0, one launch (start us, length us, event | category | flops | bytes accessed | tf_op | source)
XLA Modules:
  0.0 893.1 jit_solution(6082488349117285246)
XLA Ops:
  13.6 48.1 %all-gather.8.cloned.1.call-done = bf16[2048,512]{1,0:T(8,128)(2,1)} async-done(((bf16[512,512]{1,0:T(8,128)(2,1)}), bf16[2048,512]{1,0:T(8,128)(2,1)}) %all-gather.8.cloned.1.call-update) | async-done | bytes 2097168 | tf_op jit(solution)/shard_map/all_gather | solution.py:181
  70.3 66.4 %while.33 = (s32[]{:T(128)}, f32[4,512,2,64]{1,0,3,2:T(4,128)}, f32[4,2,512]{2,1,0:T(2,128)}, s32[4]{0:T(128)S(1)}, bf16[2112,2,64]{0,2,1:T(8,128)(2,1)S(1)}, /*...) while((s32[]{:T(128)}, f32[4,512,2,64]{1,0,3,2:T(4,128)}, ...), condition=%wide.region_5.6_spmd, body=%wide.region_2.5_spmd.sunk | while | flops 160140160 | bytes 10071036 | solution.py:95
  80.7 6.1 dynamic_update_slice.52
  97.3 6.1 dynamic_update_slice.52
  113.9 6.1 dynamic_update_slice.52
  130.5 6.1 dynamic_update_slice.52
  151.2 73.6 %reduce-scatter.5.cloned.1.call-done = f32[512,512]{1,0:T(8,128)} async-done(((f32[2048,512]{1,0:T(8,128)}), f32[512,512]{1,0:T(8,128)}) %reduce-scatter.5.cloned.1.call-update) | async-done | bytes 1048592 | tf_op jit(solution)/shard_map/reduce_scatter | solution.py:198
  227.5 45.9 %all-gather.12.cloned.1.call-done = bf16[2048,512]{1,0:T(8,128)(2,1)} async-done(((bf16[512,512]{1,0:T(8,128)(2,1)}), bf16[2048,512]{1,0:T(8,128)(2,1)}) %all-gather.12.cloned.1.call-update) | async-done | bytes 2097168 | tf_op jit(solution)/shard_map/all_gather | solution.py:216
  273.4 4.8 fusion.198
  278.3 41.9 %all-gather.10.cloned.1.call-done = bf16[2048,512]{1,0:T(8,128)(2,1)} async-done(((bf16[512,512]{1,0:T(8,128)(2,1)}), bf16[2048,512]{1,0:T(8,128)(2,1)}) %all-gather.10.cloned.1.call-update) | async-done | bytes 2097168 | tf_op jit(solution)/shard_map/all_gather | solution.py:206
  320.2 6.9 fusion.53
  331.8 5.9 fusion.187
  337.8 69.6 %reduce-scatter.9.cloned.1.call-done = f32[512,512]{1,0:T(8,128)} async-done(((f32[2048,512]{1,0:T(8,128)}), f32[512,512]{1,0:T(8,128)}) %reduce-scatter.9.cloned.1.call-update) | async-done | bytes 1048592 | tf_op jit(solution)/shard_map/reduce_scatter | solution.py:220
  409.6 77.2 %reduce-scatter.7.cloned.1.call-done = f32[512,512]{1,0:T(8,128)} async-done(((f32[2048,512]{1,0:T(8,128)}), f32[512,512]{1,0:T(8,128)}) %reduce-scatter.7.cloned.1.call-update) | async-done | bytes 1048592 | tf_op jit(solution)/shard_map/reduce_scatter | solution.py:210
  496.8 4.9 fusion.186
  502.7 34.5 %all-gather.14.cloned.1.call-done = bf16[2048,512]{1,0:T(8,128)(2,1)} async-done(((bf16[512,512]{1,0:T(8,128)(2,1)}), bf16[2048,512]{1,0:T(8,128)(2,1)}) %all-gather.14.cloned.1.call-update) | async-done | bytes 2097168 | tf_op jit(solution)/shard_map/all_gather | solution.py:225
  549.5 50.3 %while.34 = (s32[]{:T(128)}, f32[2048,2,64]{0,2,1:T(8,128)}, f32[2112,2,64]{0,2,1:T(8,128)}, f32[2112,2,64]{0,2,1:T(8,128)S(1)}, bf16[2112,2,64]{0,2,1:T(8,128)(...) while((s32[]{:T(128)}, f32[2048,2,64]{0,2,1:T(8,128)}, ...), condition=%wide.region_16.17_spmd, body=%wide.region_14.16_spmd.sunk | while | flops 385149824 | bytes 24149072 | solution.py:147
  624.2 66.9 %all-reduce.4.cloned.1.call-done = f32[96,64,128]{2,1,0:T(8,128)} async-done(((f32[96,64,128]{2,1,0:T(8,128)}), f32[96,64,128]{2,1,0:T(8,128)}) %all-reduce.4.cloned.1.call-update) | async-done | bytes 3145744 | tf_op jit(solution)/shard_map/psum | solution.py:283
  693.6 4.2 fusion.189
  698.2 4.5 fusion.140
  702.7 27.7 %all-gather.16.cloned.1.call-done = bf16[192,64,128]{2,1,0:T(8,128)(2,1)} async-done(((bf16[24,64,128]{2,1,0:T(8,128)(2,1)}), bf16[192,64,128]{2,1,0:T(8,128)(2,1)}) %all-gather.16.cloned.1.call-update) | async-done | bytes 3145744 | tf_op jit(solution)/shard_map/all_gather | solution.py:295
  730.3 3.9 gather_fusion.1
  740.4 68.8 %reduce-scatter.11.cloned.1.call-done = f32[512,512]{1,0:T(8,128)} async-done(((f32[2048,512]{1,0:T(8,128)}), f32[512,512]{1,0:T(8,128)}) %reduce-scatter.11.cloned.1.call-update) | async-done | bytes 1048592 | tf_op jit(solution)/shard_map/reduce_scatter | solution.py:243
  812.8 69.6 %all-gather.1 = f32[32,4,512]{2,1,0:T(4,128)S(1)} all-gather(f32[1,4,512]{2,1,0:T(4,128)S(1)} %maximum_bitcast_fusion), channel_id=2, replica_groups=mesh['dp'=8,'mp'=4] {'dp','mp'}, dimensions={0}, use_global_device_ids=true | all-gather | bytes 270336 | tf_op jit(solution)/shard_map/all_gather | solution.py:262
  (320 shorter events, 177.2 us)
Async XLA Ops:
  7.2 313.0 %copy-start = (bf16[512,512]{1,0:T(8,128)(2,1)S(1)}, bf16[512,512]{1,0:T(8,128)(2,1)}, u32[]{:S(2)}) copy-start(bf16[512,512]{1,0:T(8,128)(2,1)} %param.25) | copy-start | bytes 1572868
  7.2 54.4 %all-gather.8.cloned.1.call-start = ((), (), s32[]{:S(2)}) async-start(), calls=%async_computation.4 | async-start | bytes 2621440 | tf_op jit(solution)/shard_map/all_gather | solution.py:181
  10.7 215.7 %copy-start.35 = (f32[1,512]{1,0:T(1,128)}, f32[1,512]{1,0:T(1,128)S(1)}, u32[]{:S(2)}) copy-start(f32[1,512]{1,0:T(1,128)S(1)} %get-tuple-element.443) | copy-start | bytes 6148
  10.7 476.1 %copy-start.25 = (f32[1,512]{1,0:T(1,128)}, f32[1,512]{1,0:T(1,128)S(1)}, u32[]{:S(2)}) copy-start(f32[1,512]{1,0:T(1,128)S(1)} %get-tuple-element.434) | copy-start | bytes 6148
  12.8 211.9 %reduce-scatter.5.cloned.1.call-start = ((), (), s32[]{:S(2)}) async-start(), calls=%async_computation.5 | async-start | bytes 5242880 | tf_op jit(solution)/shard_map/reduce_scatter | solution.py:198
  149.1 75.7 %copy-start.2 = (bf16[1,512,512]{2,1,0:T(8,128)(2,1)S(1)}, bf16[1,512,512]{2,1,0:T(8,128)(2,1)}, u32[]{:S(2)}) copy-start(bf16[1,512,512]{2,1,0:T(8,128)(2,1)} %param.19) | copy-start | bytes 1572868
  149.1 124.3 %all-gather.12.cloned.1.call-start = ((), (), s32[]{:S(2)}) async-start(), calls=%async_computation.8 | async-start | bytes 2621440 | tf_op jit(solution)/shard_map/all_gather | solution.py:216
  150.1 339.5 %copy-start.29 = (f32[512]{0:T(512)}, f32[512]{0:T(512)S(1)}, u32[]{:S(2)}) copy-start(f32[512]{0:T(512)S(1)} %fusion.167) | copy-start | bytes 6148
  151.1 122.3 %copy-start.20 = (bf16[512,512]{1,0:T(8,128)(2,1)S(1)}, bf16[512,512]{1,0:T(8,128)(2,1)}, u32[]{:S(2)}) copy-start(bf16[512,512]{1,0:T(8,128)(2,1)} %param.26) | copy-start | bytes 1572868
  151.1 169.1 %all-gather.10.cloned.1.call-start = ((), (), s32[]{:S(2)}) async-start(), calls=%async_computation.6 | async-start | bytes 2621440 | tf_op jit(solution)/shard_map/all_gather | solution.py:206
  227.5 179.9 %reduce-scatter.9.cloned.1.call-start = ((), (), s32[]{:S(2)}) async-start(), calls=%async_computation.9 | async-start | bytes 5242880 | tf_op jit(solution)/shard_map/reduce_scatter | solution.py:220
  331.7 155.1 %reduce-scatter.7.cloned.1.call-start = ((), (), s32[]{:S(2)}) async-start(), calls=%async_computation.7 | async-start | bytes 5242880 | tf_op jit(solution)/shard_map/reduce_scatter | solution.py:210
  337.7 199.5 %all-gather.14.cloned.1.call-start = ((), (), s32[]{:S(2)}) async-start(), calls=%async_computation.10 | async-start | bytes 2621440 | tf_op jit(solution)/shard_map/all_gather | solution.py:225
  409.6 80.0 %copy-start.11 = (bf16[1,512,512]{2,1,0:T(8,128)(2,1)S(1)}, bf16[1,512,512]{2,1,0:T(8,128)(2,1)}, u32[]{:S(2)}) copy-start(bf16[1,512,512]{2,1,0:T(8,128)(2,1)} %param.20) | copy-start | bytes 1572868
  490.7 200.4 %all-reduce.4.cloned.1.call-start = ((), (), s32[]{:S(2)}) async-start(), calls=%async_computation.12 | async-start | bytes 6291456 | tf_op jit(solution)/shard_map/psum | solution.py:283
  622.7 107.6 %all-gather.16.cloned.1.call-start = ((), (), s32[]{:S(2)}) async-start(), calls=%async_computation.13 | async-start | bytes 3538944 | tf_op jit(solution)/shard_map/all_gather | solution.py:295
  697.8 111.5 %reduce-scatter.11.cloned.1.call-start = ((), (), s32[]{:S(2)}) async-start(), calls=%async_computation.11 | async-start | bytes 5242880 | tf_op jit(solution)/shard_map/reduce_scatter | solution.py:243
  739.3 143.2 %copy-start.26 = (f32[1,512]{1,0:T(1,128)S(1)}, f32[1,512]{1,0:T(1,128)}, u32[]{:S(2)}) copy-start(f32[1,512]{1,0:T(1,128)} %copy-done.25) | copy-start | bytes 6148
  739.3 143.2 %copy-start.34 = (f32[1,512]{1,0:T(1,128)S(1)}, f32[1,512]{1,0:T(1,128)}, u32[]{:S(2)}) copy-start(f32[1,512]{1,0:T(1,128)} %copy-done.33) | copy-start | bytes 6148
  739.3 143.2 %copy-start.36 = (f32[1,512]{1,0:T(1,128)S(1)}, f32[1,512]{1,0:T(1,128)}, u32[]{:S(2)}) copy-start(f32[1,512]{1,0:T(1,128)} %copy-done.35) | copy-start | bytes 6148
  739.3 143.2 %copy-start.42 = (f32[4,512]{1,0:T(4,128)S(1)}, f32[4,512]{1,0:T(4,128)}, u32[]{:S(2)}) copy-start(f32[4,512]{1,0:T(4,128)} %param.33) | copy-start | bytes 24580
  739.3 143.2 %copy-start.43 = (f32[4,512]{1,0:T(4,128)S(1)}, f32[4,512]{1,0:T(4,128)}, u32[]{:S(2)}) copy-start(f32[4,512]{1,0:T(4,128)} %param.32) | copy-start | bytes 24580
  739.3 143.9 %copy-start.30 = (f32[512]{0:T(512)S(1)}, f32[512]{0:T(512)}, u32[]{:S(2)}) copy-start(f32[512]{0:T(512)} %copy-done.29) | copy-start | bytes 6148
  739.3 143.8 %copy-start.38 = (f32[512]{0:T(512)S(1)}, f32[512]{0:T(512)}, u32[]{:S(2)}) copy-start(f32[512]{0:T(512)} %copy-done.37) | copy-start | bytes 6148
  (47 other events, 1073.6 us)
Sparse Core Ops, SparseCore 0:
  13.0 48.6 all-gather.7
  149.2 75.4 reduce-scatter.4
  227.0 46.4 all-gather.11
  275.5 44.6 all-gather.9
  331.9 75.4 reduce-scatter.8
  409.5 77.2 reduce-scatter.6
  490.8 46.3 all-gather.13
  622.9 68.1 all-reduce.3
  697.9 32.3 all-gather.15
  732.5 76.7 reduce-scatter.10
